TPU v7x, 32 devices: a whole 2x2x4 slice. The times are simulated.
32 devices in a mesh: fsdp: 4 (over y, x), dp: 8 (over z, core).
Axes of the slice: x: 2, y: 2, z: 4, core: 2. Of those that a mesh axis runs over, the one named last changes fastest.
Arguments:
- tokens: bfloat16 [16384, 1152], P(('fsdp', 'dp')), may hold values from -6 to 6
- conditions: bfloat16 [64, 1152], P(('fsdp', 'dp')), may hold values from -6 to 6
- cotangent: bfloat16 [16384, 1152], P(('fsdp', 'dp')), may hold values from -6 to 6
- slot_mask: int32 [64], P(('fsdp', 'dp')), may hold values from 0 to 1, as said below
- weight_flat: bfloat16 [186624, 128], P(('fsdp', 'dp')), may hold values from -3 to 3
- bias_flat: bfloat16 [17664], P(('fsdp', 'dp')), may hold values from -2 to 2
Outputs:
- out: bfloat16 [16384, 1152], P(('fsdp', 'dp'))
- grad_tokens: float32 [16384, 1152], P(('fsdp', 'dp'))
- grad_conditions: float32 [64, 1152], P(('fsdp', 'dp'))
- grad_weights: float32 [186624, 128], P(('fsdp', 'dp'))
- grad_biases: float32 [17664], P(('fsdp', 'dp'))
Inputs may be any that keep to these rules, and one draw needn't show every extreme that they name: `slot_mask`: on each device's 2 image slots the live ones come first; a device has one live image or all 2, and some device has all 2 live in every draw.
All inputs are finite; a program needn't handle non-finite values.
Results may differ from a plain program's by a relative error of at most 0.0095.
Values may be sent and summed in bfloat16 or wider, within the bound.
No kernel may reach another device: no remote copies, remote signals or barrier semaphores. Data moves between devices by JAX's collectives and lax.ppermute only.
A program may use at most 576 MiB of HBM per device.

v0:
```python
import math
import jax
import jax.numpy as jnp
from jax import lax
from jax.sharding import PartitionSpec as P

D = 1152
HEADS = 16
HEAD_DIM = 72
FF = 3072
GRID = 16
eps_norm = 1e-06


def unpack_weights(weight_all, bias_all):
    flat = weight_all.reshape(-1)
    layouts = ((D, 3 * D), (D, D), (D, 2 * FF), (D, 6 * D), (FF, D))
    pieces = []
    offset = 0
    for layout in layouts:
        amount = layout[0] * layout[1]
        pieces.append(flat[offset : offset + amount].reshape(layout))
        offset = offset + amount
    offset = 0
    for amount in (3 * D, D, 2 * FF, 6 * D):
        pieces.append(bias_all[offset : offset + amount])
        offset = offset + amount
    return tuple(pieces)


def rope_tables():
    quarter = HEAD_DIM // 4
    places = jnp.arange(GRID * GRID, dtype=jnp.int32)
    rows_at = (places // GRID).astype(jnp.float32)
    cols_at = (places % GRID).astype(jnp.float32)
    freqs = 10000.0 ** (-jnp.arange(quarter, dtype=jnp.float32) / quarter)
    along_rows = rows_at[:, None] * freqs[None, :]
    along_cols = cols_at[:, None] * freqs[None, :]
    angles = jnp.concatenate([along_rows, along_rows, along_cols, along_cols], axis=1)
    return (jnp.cos(angles)[:, None, :], jnp.sin(angles)[:, None, :])


def turn_half(values):
    quarter = values.shape[-1] // 4
    first = values[..., :quarter]
    second = values[..., quarter : 2 * quarter]
    third = values[..., 2 * quarter : 3 * quarter]
    fourth = values[..., 3 * quarter :]
    return jnp.concatenate([-second, first, -fourth, third], axis=-1)


def norm_parts(values):
    centred = values - jnp.mean(values, -1, keepdims=True)
    inverse = lax.rsqrt(jnp.mean(centred * centred, -1, keepdims=True) + eps_norm)
    return (centred * inverse, inverse)


def norm_back(grad_normed, normed, inverse):
    return inverse * (
        grad_normed
        - jnp.mean(grad_normed, -1, keepdims=True)
        - normed * jnp.mean(grad_normed * normed, -1, keepdims=True)
    )


def rms_parts(values):
    inverse = lax.rsqrt(jnp.mean(values * values, -1, keepdims=True) + eps_norm)
    return (values * inverse, inverse)


def rms_back(grad_normed, normed, inverse):
    return inverse * (grad_normed - normed * jnp.mean(grad_normed * normed, -1, keepdims=True))


def on_device(tokens, conditions, cotangent, slot_mask, weight_flat, bias_flat):
    f32 = jnp.float32
    bf16 = jnp.bfloat16
    slots = conditions.shape[0]
    length = GRID * GRID
    rows_all = slots * length
    scale = 1.0 / math.sqrt(HEAD_DIM)
    heads_shape = (slots, length, HEADS, HEAD_DIM)
    weight_all, bias_all = (
        lax.all_gather(weight_flat, ("fsdp", "dp"), axis=0, tiled=True),
        lax.all_gather(bias_flat, ("fsdp", "dp"), axis=0, tiled=True),
    )
    (
        query_key_value_weight,
        projection_weight,
        feedforward_weight,
        w_ada,
        down_weight,
        query_key_value_bias,
        projection_bias,
        feedforward_bias,
        b_ada,
    ) = unpack_weights(weight_all, bias_all)
    cosines, sines = rope_tables()
    mask_f = slot_mask.astype(f32)[:, None, None]
    x_f = tokens.astype(f32).reshape(slots, length, D)
    cond_f = conditions.astype(f32)
    cond_act = jax.nn.silu(cond_f).astype(bf16)
    modulation = jnp.dot(cond_act, w_ada, preferred_element_type=f32) + b_ada.astype(f32)
    shift_a, scale_a, gate_a, shift_b, scale_b, gate_b = [
        modulation[:, None, place * D : (place + 1) * D] for place in range(6)
    ]
    normed_a, inv_a = norm_parts(x_f)
    attention_input = (normed_a * (1.0 + scale_a) + shift_a).astype(bf16).reshape(rows_all, D)
    projected_output = (
        jnp.dot(attention_input, query_key_value_weight, preferred_element_type=f32)
        + query_key_value_bias.astype(f32)
    ).reshape(slots, length, 3 * D)
    q_norm, inv_q = rms_parts(projected_output[..., :D].reshape(heads_shape))
    k_norm, inv_k = rms_parts(projected_output[..., D : 2 * D].reshape(heads_shape))
    queries = (q_norm * cosines + turn_half(q_norm) * sines).astype(bf16)
    keys = (k_norm * cosines + turn_half(k_norm) * sines).astype(bf16)
    values = projected_output[..., 2 * D :].reshape(heads_shape).astype(bf16)
    scores = jnp.einsum("slhe,smhe->shlm", queries, keys, preferred_element_type=f32) * scale
    row_max = jnp.max(scores, -1, keepdims=True)
    log_total = row_max + jnp.log(jnp.sum(jnp.exp(scores - row_max), -1, keepdims=True))
    probs_low = jnp.exp(scores - log_total).astype(bf16)
    attention_output = (
        jnp.einsum("shlm,smhe->slhe", probs_low, values, preferred_element_type=f32)
        .astype(bf16)
        .reshape(rows_all, D)
    )
    attention_branch = (
        jnp.dot(attention_output, projection_weight, preferred_element_type=f32)
        + projection_bias.astype(f32)
    ).reshape(slots, length, D)
    middle = x_f + gate_a * attention_branch
    normed_b, inv_b = norm_parts(middle)
    feedforward_input = (normed_b * (1.0 + scale_b) + shift_b).astype(bf16).reshape(rows_all, D)
    mixed_tokens = jnp.dot(
        feedforward_input, feedforward_weight, preferred_element_type=f32
    ) + feedforward_bias.astype(f32)
    gate_part = mixed_tokens[:, :FF]
    up_part = mixed_tokens[:, FF:]
    hidden_state = (jax.nn.silu(gate_part) * up_part).astype(bf16)
    feedforward_branch = jnp.dot(hidden_state, down_weight, preferred_element_type=f32).reshape(
        slots, length, D
    )
    out = ((middle + gate_b * feedforward_branch) * mask_f).astype(bf16).reshape(rows_all, D)
    weight_all, bias_all = (
        lax.all_gather(weight_flat, ("fsdp", "dp"), axis=0, tiled=True),
        lax.all_gather(bias_flat, ("fsdp", "dp"), axis=0, tiled=True),
    )
    (
        query_key_value_weight,
        projection_weight,
        feedforward_weight,
        w_ada,
        down_weight,
        query_key_value_bias,
        projection_bias,
        feedforward_bias,
        b_ada,
    ) = unpack_weights(weight_all, bias_all)
    g_out = cotangent.astype(f32).reshape(slots, length, D) * mask_f
    g_branch_b = (gate_b * g_out).astype(bf16).reshape(rows_all, D)
    g_gate_b = jnp.sum(g_out * feedforward_branch, axis=1)
    grad_down = jnp.einsum("rf,rd->fd", hidden_state, g_branch_b, preferred_element_type=f32)
    g_hidden = jnp.einsum("rd,fd->rf", g_branch_b, down_weight, preferred_element_type=f32)
    sigma_gate = jax.nn.sigmoid(gate_part)
    g_mixed = jnp.concatenate(
        [
            g_hidden * up_part * sigma_gate * (1.0 + gate_part * (1.0 - sigma_gate)),
            g_hidden * (gate_part * sigma_gate),
        ],
        axis=1,
    ).astype(bf16)
    grad_mlp = jnp.einsum("rd,rf->df", feedforward_input, g_mixed, preferred_element_type=f32)
    grad_b_mlp = jnp.sum(g_mixed.astype(f32), axis=0)
    g_input_b = jnp.einsum(
        "rf,df->rd", g_mixed, feedforward_weight, preferred_element_type=f32
    ).reshape(slots, length, D)
    g_shift_b = jnp.sum(g_input_b, axis=1)
    g_scale_b = jnp.sum(g_input_b * normed_b, axis=1)
    g_middle = g_out + norm_back(g_input_b * (1.0 + scale_b), normed_b, inv_b)
    g_branch_a = (gate_a * g_middle).astype(bf16).reshape(rows_all, D)
    g_gate_a = jnp.sum(g_middle * attention_branch, axis=1)
    grad_w_out = jnp.einsum("rd,re->de", attention_output, g_branch_a, preferred_element_type=f32)
    grad_b_out = jnp.sum(g_branch_a.astype(f32), axis=0)
    g_attended = (
        jnp.einsum("re,de->rd", g_branch_a, projection_weight, preferred_element_type=f32)
        .astype(bf16)
        .reshape(heads_shape)
    )
    scores = jnp.einsum("slhe,smhe->shlm", queries, keys, preferred_element_type=f32) * scale
    probs = jnp.exp(scores - log_total)
    probs_low = probs.astype(bf16)
    g_probs = jnp.einsum("slhe,smhe->shlm", g_attended, values, preferred_element_type=f32)
    g_values = jnp.einsum("shlm,slhe->smhe", probs_low, g_attended, preferred_element_type=f32)
    g_scores = (probs * (g_probs - jnp.sum(probs * g_probs, -1, keepdims=True))).astype(bf16)
    g_queries = jnp.einsum("shlm,smhe->slhe", g_scores, keys, preferred_element_type=f32) * scale
    g_keys = jnp.einsum("shlm,slhe->smhe", g_scores, queries, preferred_element_type=f32) * scale
    g_q = rms_back(g_queries * cosines - turn_half(g_queries) * sines, q_norm, inv_q)
    g_k = rms_back(g_keys * cosines - turn_half(g_keys) * sines, k_norm, inv_k)
    g_projected = jnp.concatenate(
        [g_q.reshape(rows_all, D), g_k.reshape(rows_all, D), g_values.reshape(rows_all, D)], axis=1
    ).astype(bf16)
    grad_qkv = jnp.einsum("rd,re->de", attention_input, g_projected, preferred_element_type=f32)
    grad_b_qkv = jnp.sum(g_projected.astype(f32), axis=0)
    g_input_a = jnp.einsum(
        "re,de->rd", g_projected, query_key_value_weight, preferred_element_type=f32
    ).reshape(slots, length, D)
    g_shift_a = jnp.sum(g_input_a, axis=1)
    g_scale_a = jnp.sum(g_input_a * normed_a, axis=1)
    grad_tokens = g_middle + norm_back(g_input_a * (1.0 + scale_a), normed_a, inv_a)
    g_modulation = jnp.concatenate(
        [g_shift_a, g_scale_a, g_gate_a, g_shift_b, g_scale_b, g_gate_b], axis=1
    ).astype(bf16)
    grad_ada = jnp.einsum("sd,se->de", cond_act, g_modulation, preferred_element_type=f32)
    grad_b_ada = jnp.sum(g_modulation.astype(f32), axis=0)
    g_cond = jnp.einsum("se,de->sd", g_modulation, w_ada, preferred_element_type=f32)
    sigma_cond = jax.nn.sigmoid(cond_f)
    grad_conditions = g_cond * sigma_cond * (1.0 + cond_f * (1.0 - sigma_cond))
    narrow_count = lax.axis_size("fsdp")
    wide_count = lax.axis_size("dp")
    grads_big = jnp.concatenate(
        [
            grad_qkv.reshape(-1),
            grad_w_out.reshape(-1),
            grad_mlp.reshape(-1),
            grad_ada.reshape(-1),
            grad_down.reshape(-1),
        ]
    ).reshape(narrow_count, wide_count, -1, 128)
    grads_small = jnp.concatenate([grad_b_qkv, grad_b_out, grad_b_mlp, grad_b_ada]).reshape(
        narrow_count, wide_count, -1
    )
    spread_big, spread_small = (
        lax.all_to_all(
            lax.all_to_all(
                grads_big.astype(jnp.bfloat16), "fsdp", split_axis=0, concat_axis=0, tiled=True
            ),
            "dp",
            split_axis=1,
            concat_axis=1,
            tiled=True,
        ).astype(grads_big.dtype),
        lax.all_to_all(
            lax.all_to_all(
                grads_small.astype(jnp.bfloat16), "fsdp", split_axis=0, concat_axis=0, tiled=True
            ),
            "dp",
            split_axis=1,
            concat_axis=1,
            tiled=True,
        ).astype(grads_small.dtype),
    )
    part_weights = jnp.sum(spread_big, axis=(0, 1))
    part_biases = jnp.sum(spread_small, axis=(0, 1))
    return (out, grad_tokens.reshape(rows_all, D), grad_conditions, part_weights, part_biases)


def solution(mesh):
    return jax.shard_map(
        on_device,
        mesh=mesh,
        in_specs=(
            P(("fsdp", "dp"), None),
            P(("fsdp", "dp"), None),
            P(("fsdp", "dp"), None),
            P(("fsdp", "dp")),
            P(("fsdp", "dp"), None),
            P(("fsdp", "dp")),
        ),
        out_specs=(
            P(("fsdp", "dp"), None),
            P(("fsdp", "dp"), None),
            P(("fsdp", "dp"), None),
            P(("fsdp", "dp"), None),
            P(("fsdp", "dp")),
        ),
        check_vma=False,
    )
```

profile of v0, /device:TPU:0, one launch (start us, length us, event | category | flops | bytes accessed | tf_op | source)
XLA Modules:
  0.0 2413.1 jit_solution(1016306333423830473)
XLA Ops:
  13.1 45.2 %all-reduce = bf16[17664]{0:T(1024)(128)(2,1)S(1)} all-reduce(bf16[17664]{0:T(1024)(128)(2,1)S(1)} %dynamic-update-slice), channel_id=1, replica_groups=mesh['fsdp'=4,'dp'=8] {'fsdp','dp'}, use_global_device_ids=true, to_apply=%add | all-reduce | flops 17664 | bytes 70656
  60.6 217.3 %all-gather.2.cloned.1.call-done = bf16[186624,128]{1,0:T(8,128)(2,1)} async-done(((bf16[5832,128]{1,0:T(8,128)(2,1)}), bf16[186624,128]{1,0:T(8,128)(2,1)}) %all-gather.2.cloned.1.call-update) | async-done | bytes 47775760 | tf_op jit(solution)/shard_map/all_gather | solution.py:84
  284.3 14.0 reshape.431
  298.3 14.0 reshape.415
  319.1 15.2 reshape.433
  334.3 15.2 reshape.407
  349.5 13.4 slice.155
  362.9 29.2 %reshape.406 = bf16[1152,6912]{1,0:T(8,128)(2,1)} reshape(bf16[62208,128]{1,0:T(8,128)(2,1)} %slice.155) | data formatting | bytes 31850496 | tf_op jit(solution)/shard_map/reshape | solution.py:22
  409.9 12.8 slice.178
  422.7 20.3 reshape.432
  443.0 20.3 reshape.414
  508.5 15.8 convolution_add_fusion
  524.2 13.0 multiply_convert_fusion.2
  551.4 17.1 multiply_reduce_fusion.3
  639.6 10.5 fusion
  681.0 13.6 reshape.428
  698.9 15.9 reshape.424
  714.8 13.9 copy.106
  728.7 30.9 %reshape.427 = bf16[7962624]{0:T(1024)(128)(2,1)} reshape(bf16[1152,6912]{1,0:T(8,128)(2,1)} %convolution_convert_fusion) | data formatting | bytes 31850496 | tf_op jit(solution)/shard_map/reshape | solution.py:225
  790.7 11.6 all-to-all-start
  802.9 514.4 %all-to-all-done = bf16[4,8,5832,128]{3,2,1,0:T(8,128)(2,1)} async-done(((bf16[4,8,5832,128]{3,2,1,0:T(8,128)(2,1)}), bf16[4,8,5832,128]{3,2,1,0:T(8,128)(2,1)}, u32[]{:S(2)}, u32[]{:S(2)}) %all-to-all-start) | async-done | bytes 47775776 | tf_op jit(solution)/shard_map/all_to_all | solution.py:234
  1320.7 32.0 %copy.93 = bf16[4,8,5832,128]{3,2,0,1:T(8,128)(2,1)} copy(bf16[4,8,5832,128]{3,2,1,0:T(8,128)(2,1)} %all-to-all-done) | data formatting | bytes 95551488 | tf_op jit(solution)/shard_map/all_to_all | solution.py:234
  1372.0 1017.0 %all-to-all-done.1 = bf16[4,8,5832,128]{3,2,0,1:T(8,128)(2,1)} async-done(((bf16[4,8,5832,128]{3,2,0,1:T(8,128)(2,1)}), bf16[4,8,5832,128]{3,2,0,1:T(8,128)(2,1)}, u32[]{:S(2)}, u32[]{:S(2)}) %all-to-all-start.1) | async-done | bytes 47775776 | tf_op jit(solution)/shard_map/all_to_all | solution.py:233
  2389.0 17.1 convert_reduce_fusion
  (290 shorter events, 258.1 us)
Async XLA Ops:
  7.2 270.7 %all-gather.2.cloned.1.call-start = ((), (), s32[]{:S(2)}) async-start(), calls=%async_computation.4 | async-start | bytes 49268736 | tf_op jit(solution)/shard_map/all_gather | solution.py:84
  362.9 29.2 %copy-start.55 = (bf16[2,1152]{1,0:T(2,128)(2,1)S(1)}, bf16[2,1152]{1,0:T(2,128)(2,1)}, u32[]{:S(2)}) copy-start(bf16[2,1152]{1,0:T(2,128)(2,1)} %param.7) | copy-start | bytes 13828
  392.1 9.2 copy-start.22
  508.4 15.8 copy-start.35
  508.4 15.8 copy-start.37
  508.5 34.1 %slice-start.8 = ((s8[7077888]{0:T(1024)(128)(4,1)}), s8[4194304]{0:T(1024)(128)(4,1)S(1)}, s32[]{:S(2)}) async-start(s8[7077888]{0:T(1024)(128)(4,1)} %bitcast.165), calls=%async_computation.13 | async-start | bytes 8388608
  524.2 18.3 slice-start.9
  596.9 10.6 slice-start
  602.3 9.7 copy-start.14
  639.6 10.5 copy-start.15
  655.6 9.4 copy-start.6
  655.6 9.4 copy-start.21
  655.6 9.4 copy-start.63
  655.6 9.4 copy-start.64
  681.0 13.6 copy-start.58
  681.0 13.6 copy-start.60
  695.4 95.3 %all-to-all-start.2 = ((bf16[4,8,552]{2,1,0:T(8,128)(2,1)}), bf16[4,8,552]{2,1,0:T(8,128)(2,1)S(1)}, u32[]{:S(2)}, u32[]{:S(2)}) async-start(bf16[4,8,552]{2,1,0:T(8,128)(2,1)} %convert_element_type.155), calls=%async_computation.2 | async-start | bytes 81920 | tf_op jit(solution)/shard_map/all_to_all | solution.py:243
  759.6 11.3 copy-start.4
  766.8 11.2 slice-start.2
  770.9 9.6 slice-start.5
  770.9 16.4 slice-start.6
  790.7 526.7 %all-to-all-start = ((bf16[4,8,5832,128]{3,2,1,0:T(8,128)(2,1)}), bf16[4,8,5832,128]{3,2,1,0:T(8,128)(2,1)}, u32[]{:S(2)}, u32[]{:S(2)}) async-start(bf16[4,8,5832,128]{3,2,1,0:T(8,128)(2,1)} %bitcast.151), calls=%async_computation | async-start | bytes 95551488 | tf_op jit(solution)/shard_map/all_to_all | solution.py:234
  1317.4 35.3 %all-to-all-start.3 = ((bf16[4,8,552]{2,0,1:T(4,128)(2,1)}), bf16[4,8,552]{2,0,1:T(4,128)(2,1)S(1)}, u32[]{:S(2)}, u32[]{:S(2)}) async-start(bf16[4,8,552]{2,0,1:T(4,128)(2,1)} %copy.94), calls=%async_computation.3 | async-start | bytes 81920 | tf_op jit(solution)/shard_map/all_to_all | solution.py:242
  1352.7 1036.3 %all-to-all-start.1 = ((bf16[4,8,5832,128]{3,2,0,1:T(8,128)(2,1)}), bf16[4,8,5832,128]{3,2,0,1:T(8,128)(2,1)}, u32[]{:S(2)}, u32[]{:S(2)}) async-start(bf16[4,8,5832,128]{3,2,0,1:T(8,128)(2,1)} %copy.93), calls=%async_computation.1 | async-start | bytes 95551488 | tf_op jit(solution)/shard_map/all_to_all | solution.py:233
  (64 other events, 237.0 us)
Sparse Core Ops, SparseCore 0:
  10.9 267.0 all-gather.1
where the time goes:
time: 2420 us; the launch traced here: 2410 us
  waiting for transfers between devices  1750 us (72%)
  local copies, waits for them, and re-layouts  367 us (15%)
  matrix products  146 us (6%)
  other arithmetic  63.7 us (3%)
  blocking collectives  45.2 us (2%)
  starting transfers between devices  26.8 us (1%)
    all_to_all x1, waiting for transfers between devices, on_device(): lax.all_to_all(lax.all_to_all(grads_big.astype(jnp.bfloat16), 'fsdp', spl...  1020 us
    all_to_all x1, waiting for transfers between devices, on_device(): lax.all_to_all(grads_big.astype(jnp.bfloat16), 'fsdp', split_axis=0, conc...  514 us
    all_gather x1, waiting for transfers between devices, on_device(): lax.all_gather(weight_flat, ('fsdp', 'dp'), axis=0, tiled=True)  217 us
    reshape x8, local copies, waits for them, and re-layouts, unpack_weights(): pieces.append(flat[offset:offset + amount].reshape(layout))  134 us
    unnamed x186, local copies, waits for them, and re-layouts  52.7 us
  transfers between devices with their start and end apart: 5, of which 3 were waited for; matrix products, arithmetic and copies ran while one was open for 6% of the time, Pallas kernels for 0%

commit v1 on v0

--- a/solution.py
+++ b/solution.py
@@ -10,6 +10,26 @@
 FF = 3072
 GRID = 16
 eps_norm = 1e-06
+
+
+def track_body(slab_in, k_dim):
+    w_next = list(slab_in.shape[1:])
+    w_next[k_dim] *= slab_in.shape[0]
+    return jnp.moveaxis(slab_in, 0, k_dim).reshape(w_next)
+
+
+def deliver_ports(load, bus_axis):
+    piece_out = load[None]
+    shares = jax.lax.axis_size(bus_axis)
+    for u in range(shares.bit_length() - 1):
+        extra = 1 << u
+        odd = jax.lax.ppermute(
+            piece_out, bus_axis, perm=[(dev_i, dev_i ^ extra) for dev_i in range(shares)]
+        )
+        x_now = jnp.stack([piece_out, odd])
+        everything = jax.lax.axis_index(bus_axis) >> u & 1
+        piece_out = jnp.where(everything == 0, x_now, x_now[::-1]).reshape(-1, *load.shape)
+    return piece_out
 
 
 def unpack_weights(weight_all, bias_all):
@@ -80,8 +100,12 @@
     rows_all = slots * length
     scale = 1.0 / math.sqrt(HEAD_DIM)
     heads_shape = (slots, length, HEADS, HEAD_DIM)
+
+    def open_the_orders(tile_in, vals, row_dim):
+        return track_body(deliver_ports(tile_in, vals), row_dim)
+
     weight_all, bias_all = (
-        lax.all_gather(weight_flat, ("fsdp", "dp"), axis=0, tiled=True),
+        open_the_orders(weight_flat, ("fsdp", "dp"), 0),
         lax.all_gather(bias_flat, ("fsdp", "dp"), axis=0, tiled=True),
     )
     (

time: 2420 us -> 3880 us (1.60)
  waiting for transfers between devices: 1750 us -> 2280 us
  blocking collectives: 45.2 us -> 540 us
  local copies, waits for them, and re-layouts: 367 us -> 651 us
  other arithmetic: 63.7 us -> 185 us
    ppermute x0 -> x5, waiting for transfers between devices: none -> 787 us  [deliver_ports(): jax.lax.ppermute(piece_out, bus_axis, perm=[(dev_i, dev_i ^ extra) for de...]
    unnamed x1, blocking collectives: 45.2 us -> 540 us
    slice x5 -> x9, local copies, waits for them, and re-layouts: 42.3 us -> 364 us  [unpack_weights(): pieces.append(flat[offset:offset + amount].reshape(layout))]
    all_gather x1, waiting for transfers between devices: 217 us -> 0.01 us  [on_device(): lax.all_gather(weight_flat, ('fsdp', 'dp'), axis=0, tiled=True)]
    select_n x0 -> x4, other arithmetic: none -> 68.1 us  [deliver_ports(): jnp.where(everything == 0, x_now, x_now[::-1]).reshape(-1, *load.shape)]
    another operation x1 -> x7, other arithmetic: 3.16 us -> 58.5 us  [the longest x6 54.5 us: deliver_ports(): x_now = jnp.stack([piece_out, odd])]
    reshape x8 -> x5, local copies, waits for them, and re-layouts: 134 us -> 84.8 us  [unpack_weights(): pieces.append(flat[offset:offset + amount].reshape(layout))]
    all_to_all x1, waiting for transfers between devices: 1020 us -> 975 us  [on_device(): lax.all_to_all(lax.all_to_all(grads_big.astype(jnp.bfloat16), 'fsdp', spl...]
  transfers between devices with their start and end apart: 5 -> 10, of which waited for: 3 -> 6; matrix products, arithmetic and copies ran while one was open for 6% -> 16% of each run, Pallas kernels for 0% -> 0%
where the time goes in v1:
time: 3880 us; the launch traced here: 3870 us
  waiting for transfers between devices  2280 us (59%)
  local copies, waits for them, and re-layouts  651 us (17%)
  blocking collectives  540 us (14%)
  other arithmetic  185 us (5%)
  matrix products  159 us (4%)
  starting transfers between devices  39.7 us (1%)
    all_to_all x1, waiting for transfers between devices, on_device(): lax.all_to_all(lax.all_to_all(grads_big.astype(jnp.bfloat16), 'fsdp', spl...  975 us
    ppermute x5, waiting for transfers between devices, deliver_ports(): jax.lax.ppermute(piece_out, bus_axis, perm=[(dev_i, dev_i ^ extra) for de...  787 us
    unnamed x1, blocking collectives  540 us
    all_to_all x1, waiting for transfers between devices, on_device(): lax.all_to_all(grads_big.astype(jnp.bfloat16), 'fsdp', split_axis=0, conc...  513 us
    slice x9, local copies, waits for them, and re-layouts, unpack_weights(): pieces.append(flat[offset:offset + amount].reshape(layout))  364 us
    reshape x5, local copies, waits for them, and re-layouts, unpack_weights(): pieces.append(flat[offset:offset + amount].reshape(layout))  84.8 us
  transfers between devices with their start and end apart: 10, of which 6 were waited for; matrix products, arithmetic and copies ran while one was open for 16% of the time, Pallas kernels for 0%

profile of v1, /device:TPU:0, one launch (start us, length us, event | category | flops | bytes accessed | tf_op | source)
XLA Modules:
  0.0 3865.4 jit_solution(15305956656096616226)
XLA Ops:
  17.2 142.9 %collective-permute-done.1 = bf16[2,5832,128]{2,1,0:T(8,128)(2,1)} collective-permute-done((bf16[2,5832,128]{2,1,0:T(8,128)(2,1)}, bf16[2,5832,128]{2,1,0:T(8,128)(2,1)}, u32[]{:S(2)}, u32[]{:S(2)}) %collective-permute-start.1) | collective-permute-done | bytes 2986016 | tf_op jit(solution)/shard_map/ppermute | solution.py:26
  172.4 385.5 %collective-permute-done.2 = bf16[4,5832,128]{2,1,0:T(8,128)(2,1)} collective-permute-done((bf16[4,5832,128]{2,1,0:T(8,128)(2,1)}, bf16[4,5832,128]{2,1,0:T(8,128)(2,1)}, u32[]{:S(2)}, u32[]{:S(2)}) %collective-permute-start.2) | collective-permute-done | bytes 5972000 | tf_op jit(solution)/shard_map/ppermute | solution.py:26
  571.6 255.5 %collective-permute-done.3 = bf16[8,5832,128]{2,1,0:T(8,128)(2,1)} collective-permute-done((bf16[8,5832,128]{2,1,0:T(8,128)(2,1)}, bf16[8,5832,128]{2,1,0:T(8,128)(2,1)}, u32[]{:S(2)}, u32[]{:S(2)}) %collective-permute-start.3) | collective-permute-done | bytes 11943968 | tf_op jit(solution)/shard_map/ppermute | solution.py:26
  854.5 540.5 %all-reduce = bf16[17664]{0:T(1024)(128)(2,1)S(1)} all-reduce(bf16[17664]{0:T(1024)(128)(2,1)S(1)} %dynamic-update-slice), channel_id=1, replica_groups=mesh['fsdp'=4,'dp'=8] {'fsdp','dp'}, use_global_device_ids=true, to_apply=%add | all-reduce | flops 17664 | bytes 70656
  1398.5 31.9 pad_maximum_fusion
  1430.4 46.6 %reverse_select_fusion = bf16[2,16,5832,128]{3,2,1,0:T(8,128)(2,1)} fusion(bf16[2,16,5832,128]{3,2,1,0:T(8,128)(2,1)} %pad_maximum_fusion, pred[]{:T(512)S(6)} %eq.17), kind=kLoop, calls=%fused_computation.1 | loop fusion | flops 23887872 | bytes 95551488 | tf_op jit(solution)/shard_map/jit(_where)/select_n | solution.py:31
  1477.1 84.3 %slice.142 = bf16[3456,6912]{1,0:T(8,128)(2,1)} reshape(bf16[2,16,5832,128]{3,2,1,0:T(8,128)(2,1)} %reverse_select_fusion) | data formatting | bytes 95551488 | tf_op jit(solution)/shard_map/slice | solution.py:42
  1561.4 84.6 %slice.148 = bf16[6912,3456]{1,0:T(8,128)(2,1)} reshape(bf16[2,16,5832,128]{3,2,1,0:T(8,128)(2,1)} %reverse_select_fusion) | data formatting | bytes 95551488 | tf_op jit(solution)/shard_map/slice | solution.py:42
  1645.9 87.3 %slice.162 = bf16[20736,1152]{1,0:T(8,128)(2,1)} reshape(bf16[2,16,5832,128]{3,2,1,0:T(8,128)(2,1)} %reverse_select_fusion) | data formatting | bytes 95551488 | tf_op jit(solution)/shard_map/slice | solution.py:42
  1733.3 65.4 %slice.168 = bf16[3888,6144]{1,0:T(8,128)(2,1)} reshape(bf16[2,16,5832,128]{3,2,1,0:T(8,128)(2,1)} %reverse_select_fusion) | data formatting | bytes 95551488 | tf_op jit(solution)/shard_map/slice | solution.py:42
  1855.6 14.8 fusion.4
  1876.7 14.0 reshape.438
  1903.5 20.3 reshape.457
  1948.2 17.1 multiply_reduce_fusion.3
  2047.2 15.2 reshape.458
  2127.7 15.9 reshape.449
  2155.3 14.0 copy.106
  2169.3 30.9 reshape.452
  2200.2 13.9 reshape.453
  2256.5 513.0 %all-to-all-done = bf16[4,8,5832,128]{3,2,1,0:T(8,128)(2,1)} async-done(((bf16[4,8,5832,128]{3,2,1,0:T(8,128)(2,1)}), bf16[4,8,5832,128]{3,2,1,0:T(8,128)(2,1)}, u32[]{:S(2)}, u32[]{:S(2)}) %all-to-all-start) | async-done | bytes 47775776 | tf_op jit(solution)/shard_map/all_to_all | solution.py:258
  2773.0 31.9 copy.93
  2826.6 29.0 reshape.445
  2866.6 974.6 %all-to-all-done.1 = bf16[4,8,5832,128]{3,2,0,1:T(8,128)(2,1)} async-done(((bf16[4,8,5832,128]{3,2,0,1:T(8,128)(2,1)}), bf16[4,8,5832,128]{3,2,0,1:T(8,128)(2,1)}, u32[]{:S(2)}, u32[]{:S(2)}) %all-to-all-start.1) | async-done | bytes 47775776 | tf_op jit(solution)/shard_map/all_to_all | solution.py:257
  3841.2 17.1 convert_reduce_fusion
  (317 shorter events, 403.9 us)
Async XLA Ops:
  7.2 1863.2 %all-gather.2.cloned.1.call-start = ((), (), s32[]{:S(2)}) async-start(), calls=%async_computation.4 | async-start | bytes 49268736 | tf_op jit(solution)/shard_map/all_gather | solution.py:169
  7.9 3.7 collective-permute-start
  14.2 145.8 %collective-permute-start.1 = (bf16[2,5832,128]{2,1,0:T(8,128)(2,1)}, bf16[2,5832,128]{2,1,0:T(8,128)(2,1)}, u32[]{:S(2)}, u32[]{:S(2)}) collective-permute-start(bf16[2,5832,128]{2,1,0:T(8,128)(2,1)} %get-tuple-element.26), channel_id=1, source_target_pairs={{0,2},{1,3},{2,0},{3,1},{4,6},{5,7},{6,4},{7,5},{8,10},{9,11},{10,... | collective-permute-start | bytes 8957960 | tf_op jit(solution)/shard_map/ppermute | solution.py:26
  166.2 391.7 %collective-permute-start.2 = (bf16[4,5832,128]{2,1,0:T(8,128)(2,1)}, bf16[4,5832,128]{2,1,0:T(8,128)(2,1)}, u32[]{:S(2)}, u32[]{:S(2)}) collective-permute-start(bf16[4,5832,128]{2,1,0:T(8,128)(2,1)} %bitcast.8), channel_id=1, source_target_pairs={{0,4},{1,5},{2,6},{3,7},{4,0},{5,1},{6,2},{7,3},{8,12},{9,13},{10,... | collective-permute-start | bytes 17915912 | tf_op jit(solution)/shard_map/ppermute | solution.py:26
  570.1 257.0 %collective-permute-start.3 = (bf16[8,5832,128]{2,1,0:T(8,128)(2,1)}, bf16[8,5832,128]{2,1,0:T(8,128)(2,1)}, u32[]{:S(2)}, u32[]{:S(2)}) collective-permute-start(bf16[8,5832,128]{2,1,0:T(8,128)(2,1)} %bitcast.11), channel_id=1, source_target_pairs={{0,8},{1,9},{2,10},{3,11},{4,12},{5,13},{6,14},{7,15},{8,0},{9,1},... | collective-permute-start | bytes 35831816 | tf_op jit(solution)/shard_map/ppermute | solution.py:26
  838.6 13.8 copy-start.5
  850.2 548.3 %collective-permute-start.4 = (bf16[16,5832,128]{2,1,0:T(8,128)(2,1)}, bf16[16,5832,128]{2,1,0:T(8,128)(2,1)}, u32[]{:S(2)}, u32[]{:S(2)}) collective-permute-start(bf16[16,5832,128]{2,1,0:T(8,128)(2,1)} %bitcast.14), channel_id=1, source_target_pairs={{0,16},{1,17},{2,18},{3,19},{4,20},{5,21},{6,22},{7,23},{8,24},{9,... | collective-permute-start | bytes 71663624 | tf_op jit(solution)/shard_map/ppermute | solution.py:26
  852.7 577.7 %copy-start.60 = (f32[512]{0:T(512)}, f32[512]{0:T(512)S(1)}, u32[]{:S(2)}) copy-start(f32[512]{0:T(512)S(1)} %broadcast_multiply_fusion.12) | copy-start | bytes 6148
  1733.3 65.4 %copy-start.49 = (f32[6912]{0:T(1024)S(1)}, f32[6912]{0:T(1024)}, u32[]{:S(2)}) copy-start(f32[6912]{0:T(1024)} %slice_convert_fusion.1) | copy-start | bytes 82948
  1733.3 65.4 %copy-start.52 = (bf16[2,1152]{1,0:T(2,128)(2,1)S(1)}, bf16[2,1152]{1,0:T(2,128)(2,1)}, u32[]{:S(2)}) copy-start(bf16[2,1152]{1,0:T(2,128)(2,1)} %param.7) | copy-start | bytes 13828
  1923.8 13.3 copy-start.57
  1923.8 13.3 copy-start.75
  2200.2 13.9 copy-start.55
  2200.2 13.9 copy-start.58
  2200.2 13.9 copy-start.65
  2214.8 29.5 all-to-all-start.2
  2218.4 14.8 slice-start.2
  2220.0 14.4 slice-start.5
  2220.1 21.0 slice-start.6
  2244.3 525.2 %all-to-all-start = ((bf16[4,8,5832,128]{3,2,1,0:T(8,128)(2,1)}), bf16[4,8,5832,128]{3,2,1,0:T(8,128)(2,1)}, u32[]{:S(2)}, u32[]{:S(2)}) async-start(bf16[4,8,5832,128]{3,2,1,0:T(8,128)(2,1)} %bitcast.176), calls=%async_computation | async-start | bytes 95551488 | tf_op jit(solution)/shard_map/all_to_all | solution.py:258
  2769.5 35.4 all-to-all-start.3
  2804.9 1036.3 %all-to-all-start.1 = ((bf16[4,8,5832,128]{3,2,0,1:T(8,128)(2,1)}), bf16[4,8,5832,128]{3,2,0,1:T(8,128)(2,1)}, u32[]{:S(2)}, u32[]{:S(2)}) async-start(bf16[4,8,5832,128]{3,2,0,1:T(8,128)(2,1)} %copy.93), calls=%async_computation.1 | async-start | bytes 95551488 | tf_op jit(solution)/shard_map/all_to_all | solution.py:257
  2826.6 29.1 copy-start.48
  2826.6 29.1 copy-start.54
  (73 other events, 351.4 us)
Sparse Core Ops, SparseCore 0:
  10.9 494.6 all-gather.1
